TPU v7x, 32 devices: a whole 2x2x4 slice. The times are simulated.
32 devices in a mesh: exp: 8 (over z, x), seq: 4 (over y, core).
Axes of the slice: x: 2, y: 2, z: 4, core: 2. Of those that a mesh axis runs over, the one named last changes fastest.
Arguments:
- out_grad: bfloat16 [4096, 4096], P(('exp', 'seq')), may hold values from -1.5 to 1.5
- chosen: int32 [8, 1024], P('exp'), may hold values from 0 to 4095, as said below
- scores: float32 [8, 1024], P('exp'), may hold values from 0.05 to 1
- saved_pre: bfloat16 [8, 1024, 2, 1536], P('exp', None, None, 'seq'), may hold values from -6 to 6
- gate_up: bfloat16 [8, 4096, 2, 1536], P('exp', None, None, 'seq'), may hold values from -0.09375 to 0.09375
- down: bfloat16 [8, 1536, 4096], P('exp', 'seq'), may hold values from -0.15625 to 0.15625
Outputs:
- in_grad: bfloat16 [4096, 4096], P(('exp', 'seq'))
- score_grad: float32 [8, 1024], P('exp')
Inputs may be any that keep to these rules, and one draw needn't show every extreme that they name: `chosen`: each row lists 1024 different tokens. At most 144 of one row's tokens lie in one block of 512 consecutive tokens (the tokens of one index of exp), and every row has exactly 144 in some block.
All inputs are finite; a program needn't handle non-finite values.
Results may differ from a plain program's by a relative error of at most 0.012.
Values may be sent and summed in bfloat16 or wider, within the bound.
A program may use at most 128 MiB of HBM per device.

v0:
```python
import jax
import jax.numpy as jnp
from jax import lax
from jax.sharding import PartitionSpec as P


def local(out_grad, chosen, scores, saved_pre, gate_up, down):
    n_exp = lax.axis_size("exp")
    n_seq = lax.axis_size("seq")
    capacity = chosen.shape[1]
    slot_most = 9 * capacity // (8 * n_exp)
    tok_count = out_grad.shape[0]
    model_width = out_grad.shape[1]
    group_tok = tok_count * n_seq
    pad_rows = n_exp * slot_most
    hidden_part = gate_up.shape[3]
    group_index = lax.axis_index("exp")
    all_ids = lax.all_gather(chosen, "exp", axis=0, tiled=True)
    group_grad = lax.all_gather(out_grad, "seq", axis=0, tiled=True)
    local_ids = all_ids - group_index * group_tok
    inside = (local_ids >= 0) & (local_ids < group_tok)
    slot_rank = jnp.cumsum(inside.astype(jnp.int32), axis=1) - 1
    slot_ids = jnp.arange(slot_most, dtype=jnp.int32)
    picked = inside[:, None, :] & (slot_rank[:, None, :] == slot_ids[None, :, None])
    filled = jnp.any(picked, axis=2).reshape(pad_rows)
    source_row = jnp.sum(jnp.where(picked, local_ids[:, None, :], 0), axis=2).reshape(pad_rows)
    outgoing = jnp.where(filled[:, None], group_grad[source_row], jnp.zeros((), jnp.bfloat16))
    fetched = lax.all_to_all(outgoing, "exp", split_axis=0, concat_axis=0, tiled=True)
    own_ids = chosen[0]
    owner_group = own_ids // group_tok
    owner_hits = (owner_group[:, None] == jnp.arange(n_exp, dtype=jnp.int32)[None, :]).astype(
        jnp.int32
    )
    slot_order = jnp.sum(jnp.cumsum(owner_hits, axis=0) * owner_hits, axis=1) - 1
    position = owner_group * slot_most + slot_order
    down_rows = down[0]
    mixing = gate_up[0].reshape(model_width, 2 * hidden_part)
    pre_padded = jnp.zeros((pad_rows, 2, hidden_part), jnp.bfloat16).at[position].set(saved_pre[0])
    weight_padded = jnp.zeros((pad_rows,), jnp.float32).at[position].set(scores[0])
    back_grad = lax.dot_general(
        fetched, down_rows, (((1,), (1,)), ((), ())), preferred_element_type=jnp.float32
    )
    gate_pre = pre_padded[:, 0].astype(jnp.float32)
    up_pre = pre_padded[:, 1].astype(jnp.float32)
    sigmoid_gate = jax.nn.sigmoid(gate_pre)
    activated = gate_pre * sigmoid_gate
    hidden = (activated * up_pre).astype(jnp.bfloat16)
    hidden = lax.optimization_barrier(hidden)
    score_part = jnp.sum(hidden.astype(jnp.float32) * back_grad, axis=1)
    scaled = weight_padded[:, None] * back_grad
    d_gate = scaled * up_pre * sigmoid_gate * (1.0 + gate_pre * (1.0 - sigmoid_gate))
    d_up = scaled * activated
    d_both = (
        jnp.stack([d_gate, d_up], axis=1)
        .astype(jnp.bfloat16)
        .reshape(fetched.shape[0], 2 * hidden_part)
    )
    partial_value = lax.dot_general(
        d_both, mixing, (((1,), (1,)), ((), ())), preferred_element_type=jnp.float32
    ).astype(jnp.bfloat16)
    partial_value, score_padded = (partial_value, score_part)
    score_part = score_padded[position]
    score_grad = lax.psum(score_part, "seq")[None, :]
    arrived = lax.all_to_all(partial_value, "exp", split_axis=0, concat_axis=0, tiled=True)
    totals = (
        jnp.zeros((group_tok, model_width), jnp.float32)
        .at[source_row]
        .add(arrived.astype(jnp.float32))
    )
    summed = lax.psum_scatter(totals.astype(jnp.bfloat16), "seq", scatter_dimension=0, tiled=True)
    return (summed, score_grad)


def solution(mesh):
    return jax.shard_map(
        local,
        mesh=mesh,
        in_specs=(
            P(("exp", "seq"), None),
            P("exp", None),
            P("exp", None),
            P("exp", None, None, "seq"),
            P("exp", None, None, "seq"),
            P("exp", "seq", None),
        ),
        out_specs=(P(("exp", "seq"), None), P("exp", None)),
        check_vma=False,
    )
```

profile of v0, /device:TPU:8, one launch (start us, length us, event | category | flops | bytes accessed | tf_op | source)
XLA Modules:
  0.0 610.0 jit_solution(15147982498281689753)
XLA Ops:
  7.9 28.2 %all-gather = s32[8,1,1024]{2,1,0:T(1,128)S(1)} all-gather(s32[1,1,1024]{2,1,0:T(1,128)} %bitcast.99), channel_id=1, replica_groups=mesh['exp'=8,'seq'=4] {'exp'}, dimensions={0}, use_global_device_ids=true | all-gather | bytes 36864 | tf_op jit(solution)/shard_map/all_gather | solution.py:18
  36.2 2.3 reduce-window.14
  41.0 4.2 all-gather.3.cloned.1.call-done
  45.3 21.1 %gather_fusion = bf16[1152,4096]{1,0:T(8,128)(2,1)} fusion(bf16[512,4096]{1,0:T(8,128)(2,1)} %all-gather.3.cloned.1.call-done, s32[2048]{0:T(1024)S(1)} %pad_clamp_fusion), kind=kCustom, calls=%fused_computation | custom fusion | bytes 18878976 | tf_op jit(solution)/shard_map/gather | solution.py:27
  66.4 8.0 %broadcast_select_fusion = bf16[8,144,4096]{2,1,0:T(8,128)(2,1)} fusion(bf16[8,144,4096]{2,1,0:T(8,128)(2,1)} %bitcast.87, pred[8,144]{1,0:T(8,128)(4,1)S(1)} %fusion.3), kind=kLoop, calls=%fused_computation.8 | loop fusion | flops 4718592 | bytes 18875520 | tf_op jit(solution)/shard_map/jit(_where)/select_n | solution.py:27
  74.4 6.2 %all-to-all-start = ((bf16[8,144,4096]{2,1,0:T(8,128)(2,1)}), bf16[8,144,4096]{2,1,0:T(8,128)(2,1)}, u32[]{:S(2)}, u32[]{:S(2)}) async-start(bf16[8,144,4096]{2,1,0:T(8,128)(2,1)} %broadcast_select_fusion), calls=%async_computation | async-start | bytes 18874368 | tf_op jit(solution)/shard_map/all_to_all | solution.py:28
  80.6 2.3 reduce-window.16
  83.5 2.3 broadcast_in_dim.54
  85.8 110.3 %scatter_fusion = bf16[1152,2,384]{2,1,0:T(2,128)(2,1)} fusion(bf16[1152,2,384]{2,1,0:T(2,128)(2,1)} %broadcast_in_dim.54, s32[1024]{0:T(1024)S(1)} %bitcast.102, bf16[1024,2,384]{2,1,0:T(2,128)(2,1)} %bitcast.92), kind=kCustom, calls=%fused_computation.3 | custom fusion | bytes 4722688 | tf_op jit(solution)/shard_map/scatter | solution.py:38
  196.1 6.5 %fusion.27 = (bf16[1152,1,384]{2,1,0:T(2,128)(2,1)}, bf16[1152,1,384]{2,1,0:T(2,128)(2,1)}) fusion(bf16[1152,2,384]{2,1,0:T(2,128)(2,1)} %scatter_fusion), kind=kLoop, calls=%fused_computation.76 | loop fusion | bytes 3538944 | tf_op jit(solution)/shard_map/slice | solution.py:44
  202.5 4.9 copy.18
  207.4 4.8 copy.19
  212.2 2.9 fusion.10
  215.1 6.5 %copy.22 = bf16[512,8,2,384]{3,1,2,0:T(8,128)(2,1)} copy(bf16[512,8,2,384]{3,2,1,0:T(2,128)(2,1)} %bitcast.89) | data formatting | bytes 12582912
  221.5 4.5 scatter_custom_fusion
  226.0 58.0 %all-to-all-done = bf16[8,144,4096]{2,1,0:T(8,128)(2,1)} async-done(((bf16[8,144,4096]{2,1,0:T(8,128)(2,1)}), bf16[8,144,4096]{2,1,0:T(8,128)(2,1)}, u32[]{:S(2)}, u32[]{:S(2)}) %all-to-all-start) | async-done | bytes 9437216 | tf_op jit(solution)/shard_map/all_to_all | solution.py:28
  284.1 11.3 %fusion.16 = (bf16[1152,1,384]{0,2,1:T(8,128)(2,1)S(1)}, bf16[1152,1,384]{0,2,1:T(8,128)(2,1)S(1)}, f32[1152]{0:T(1024)S(1)}) fusion(bf16[1152,1,384]{0,2,1:T(8,128)(2,1)} %copy.19, bf16[1152,1,384]{0,2,1:T(8,128)(2,1)} %copy.18, f32[1152]{0:T(1024)S(1)} %scatter_custom_fusion, bf16[1152,384]{0,1:T(8,128)(2,1)} %fusion.10, bf16[1152,4096]{1,0:T(8,128)(2,1)} %bitcast.10, ...), kind=kOutput, calls=%fused_computation.33 | convolution fusion | flops 3632282624 | bytes 17015808 | tf_op jit(solution)/shard_map/dot_general | solution.py:40
  295.6 8.2 %convolution_convert_fusion = bf16[1152,4096]{1,0:T(8,128)(2,1)S(1)} fusion(bf16[1152,768]{0,1:T(8,128)(2,1)S(1)} %bitcast.91, bf16[4096,768]{1,0:T(8,128)(2,1)S(1)} %bitcast.90), kind=kOutput, calls=%fused_computation.7 | convolution fusion | flops 7252475904 | bytes 17498112 | tf_op jit(solution)/shard_map/dot_general | solution.py:58
  303.7 210.9 %all_to_all.18 = bf16[8,144,4096]{2,1,0:T(8,128)(2,1)} all-to-all(bf16[8,144,4096]{2,1,0:T(8,128)(2,1)S(1)} %bitcast.88), channel_id=1, replica_groups=mesh['exp'=8,'seq'=4] {'exp'}, dimensions={0} | all-to-all | bytes 18874368 | tf_op jit(solution)/shard_map/all_to_all | solution.py:64
  514.6 39.5 %scatter_custom_fusion.2 = f32[512,4096]{1,0:T(8,128)} fusion(s32[1152]{0:T(1024)S(1)} %fusion.20, bf16[1152,4096]{1,0:T(8,128)(2,1)} %bitcast.86, f32[]{:T(128)} %constant.17.clone.1), kind=kCustom, calls=%fused_computation.5 | custom fusion | flops 9437184 | bytes 17825796 | tf_op jit(solution)/shard_map/scatter-add | solution.py:68
  554.1 5.9 convert_element_type.56
  560.1 6.2 %gather_fusion.1 = f32[1024]{0:T(1024)S(1)} fusion(f32[1152]{0:T(1024)S(1)} %get-tuple-element.6, s32[1024]{0:T(1024)S(1)} %broadcast_clamp_fusion), kind=kCustom, calls=%fused_computation.1 | custom fusion | bytes 12288 | tf_op jit(solution)/shard_map/gather | solution.py:62
  566.2 6.5 %psum.7 = f32[1,1024]{1,0:T(1,128)} all-reduce(f32[1,1024]{1,0:T(1,128)S(1)} %bitcast.108), channel_id=1, replica_groups=mesh['exp'=8,'seq'=4] {'seq'}, use_global_device_ids=true, to_apply=%region_12.13 | all-reduce | flops 1024 | bytes 8192 | tf_op jit(solution)/shard_map/psum | solution.py:63
  572.8 30.4 %reduce-scatter.2.cloned.1.call-done = bf16[128,4096]{1,0:T(8,128)(2,1)} async-done(((bf16[512,4096]{1,0:T(8,128)(2,1)}), bf16[128,4096]{1,0:T(8,128)(2,1)}) %reduce-scatter.2.cloned.1.call-update) | async-done | bytes 1048592 | tf_op jit(solution)/shard_map/reduce_scatter | solution.py:70
  (36 shorter events, 4.1 us)
Async XLA Ops:
  7.2 276.9 %copy-start = (bf16[1,384,4096]{2,1,0:T(8,128)(2,1)S(1)}, bf16[1,384,4096]{2,1,0:T(8,128)(2,1)}, u32[]{:S(2)}) copy-start(bf16[1,384,4096]{2,1,0:T(8,128)(2,1)} %param.11) | copy-start | bytes 9437188
  7.2 38.1 %all-gather.3.cloned.1.call-start = ((), (), s32[]{:S(2)}) async-start(), calls=%async_computation.3 | async-start | bytes 5242880 | tf_op jit(solution)/shard_map/all_gather | solution.py:19
  74.4 6.2 %copy-start.3 = (s32[1,1024]{1,0:T(1,128)S(1)}, s32[1,1024]{1,0:T(1,128)}, u32[]{:S(2)}) copy-start(s32[1,1024]{1,0:T(1,128)} %param.7) | copy-start | bytes 12292
  74.4 209.7 %all-to-all-start = ((bf16[8,144,4096]{2,1,0:T(8,128)(2,1)}), bf16[8,144,4096]{2,1,0:T(8,128)(2,1)}, u32[]{:S(2)}, u32[]{:S(2)}) async-start(bf16[8,144,4096]{2,1,0:T(8,128)(2,1)} %broadcast_select_fusion), calls=%async_computation | async-start | bytes 18874368 | tf_op jit(solution)/shard_map/all_to_all | solution.py:28
  80.6 522.6 %reduce-scatter.2.cloned.1.call-start = ((), (), s32[]{:S(2)}) async-start(), calls=%async_computation.4 | async-start | bytes 5242880 | tf_op jit(solution)/shard_map/reduce_scatter | solution.py:70
  284.1 11.5 %copy-start.2 = (bf16[512,8,2,384]{3,1,2,0:T(8,128)(2,1)S(1)}, bf16[512,8,2,384]{3,1,2,0:T(8,128)(2,1)}, u32[]{:S(2)}) copy-start(bf16[512,8,2,384]{3,1,2,0:T(8,128)(2,1)} %copy.22) | copy-start | bytes 18874372
  560.1 43.1 %copy-start.1 = (bf16[1,384,4096]{2,1,0:T(8,128)(2,1)S(1)}, bf16[1,384,4096]{2,1,0:T(8,128)(2,1)}, u32[]{:S(2)}) copy-start(bf16[1,384,4096]{2,1,0:T(8,128)(2,1)} %param.11) | copy-start | bytes 9437188
Sparse Core Ops, SparseCore 0:
  9.6 35.6 all-gather.2
  560.2 42.9 reduce-scatter.1
where the time goes:
time: 617 us; the launch traced here: 610 us
  blocking collectives  246 us (40%)
  local copies, waits for them, and re-layouts  168 us (27%)
  waiting for transfers between devices  93.4 us (15%)
  other arithmetic  63.5 us (10%)
  matrix products  19.5 us (3%)
  between operations  14.2 us (2%)
  starting transfers between devices  6.22 us (1%)
    all_to_all x1, blocking collectives, local(): lax.all_to_all(partial_value, 'exp', split_axis=0, concat_axis=0, tiled=T...  211 us
    scatter x1, local copies, waits for them, and re-layouts, local(): jnp.zeros((pad_rows, 2, hidden_part), jnp.bfloat16).at[position]  110 us
    all_to_all x1, waiting for transfers between devices, local(): lax.all_to_all(outgoing, 'exp', split_axis=0, concat_axis=0, tiled=True)  58 us
    scatter-add x1, other arithmetic, local(): totals = jnp.zeros((group_tok, model_width), jnp.float32).at[source_row]....  39.5 us
    reduce_scatter x1, waiting for transfers between devices, local(): lax.psum_scatter(totals.astype(jnp.bfloat16), 'seq', scatter_dimension=0,...  30.4 us
    all_gather x1, blocking collectives, local(): all_ids = lax.all_gather(chosen, 'exp', axis=0, tiled=True)  28.2 us
    gather x1, local copies, waits for them, and re-layouts, local(): group_grad[source_row]  21.1 us
    unnamed x13, local copies, waits for them, and re-layouts  16.2 us
  transfers between devices with their start and end apart: 3, of which 3 were waited for; matrix products, arithmetic and copies ran while one was open for 26% of the time, Pallas kernels for 0%

commit v1 on v0

v1 whole, which is shorter than its diff:
```python
import functools

import jax
import jax.numpy as jnp
from jax import lax
from jax.experimental import pallas as pl
from jax.experimental.pallas import tpu as pltpu
from jax.sharding import PartitionSpec as P

MESH = pl.DeviceIdType.MESH
ANY = pl.BlockSpec(memory_space=pl.ANY)
VMEM = pl.BlockSpec(memory_space=pltpu.VMEM)


def flip(index, bits):
    out, step = index, 1
    while bits >= step:
        if bits & step:
            out = out + step * (1 - 2 * ((index // step) % 2))
        step *= 2
    return out


def greet(peers):
    barrier = pltpu.get_barrier_semaphore()
    for p in peers:
        pl.semaphore_signal(barrier, inc=1, device_id=p, device_id_type=MESH)
    pl.semaphore_wait(barrier, len(peers))


def remote(src, dst, send, recv, to):
    return pltpu.make_async_remote_copy(
        src_ref=src, dst_ref=dst, send_sem=send, recv_sem=recv, device_id=to, device_id_type=MESH
    )


def columns(quarter, width):
    return pl.ds(pl.multiple_of(quarter * width, 128), width)


def exchange_kernel(n_exp, n_seq, chosen, grad, ids, group, send_i, recv_i, send_g, recv_g, local):
    g, s = lax.axis_index("exp"), lax.axis_index("seq")
    width = grad.shape[1] // n_seq
    greet([(flip(g, k), s) for k in range(1, n_exp)] + [(g, flip(s, k)) for k in range(1, n_seq)])
    copies = []
    for k in range(1, n_exp):
        copies.append(remote(chosen, ids.at[g], send_i.at[k], recv_i.at[k], (flip(g, k), s)))
        copies[-1].start()
    for k in range(n_seq - 1, 0, -1):
        t = flip(s, k)
        copies.append(
            remote(grad.at[:, columns(t, width)], group.at[s], send_g.at[k], recv_g.at[k], (g, t))
        )
        copies[-1].start()
    own_ids = pltpu.make_async_copy(chosen, ids.at[g], local.at[0])
    own_grad = pltpu.make_async_copy(grad.at[:, columns(s, width)], group.at[s], local.at[1])
    own_ids.start()
    own_grad.start()
    for c in copies:
        c.wait()
    own_ids.wait()
    own_grad.wait()


def exchange(n_exp, n_seq, chosen, grad):
    rows, width = grad.shape[0], grad.shape[1] // n_seq
    dma = pltpu.SemaphoreType.DMA
    return pl.pallas_call(
        functools.partial(exchange_kernel, n_exp, n_seq),
        out_shape=(
            jax.ShapeDtypeStruct((n_exp,) + chosen.shape, chosen.dtype),
            jax.ShapeDtypeStruct((n_seq, rows, width), grad.dtype),
        ),
        in_specs=[VMEM, VMEM],
        out_specs=(VMEM, VMEM),
        scratch_shapes=[dma((n_exp,)), dma((n_exp,)), dma((n_seq,)), dma((n_seq,)), dma((2,))],
        compiler_params=pltpu.CompilerParams(collective_id=0, has_side_effects=True),
    )(chosen, grad)


def dispatch_kernel(n_exp, out, fetched, s0, r0, sa, ra, sb, rb, sc, rc, local):
    g, s = lax.axis_index("exp"), lax.axis_index("seq")
    width = out.shape[2]
    across, beside = (g, flip(s, 2)), (g, flip(s, 1))
    own, theirs = columns(s, width), columns(flip(s, 2), width)
    greet([(flip(g, k), s) for k in range(1, n_exp)] + [across, beside])
    first = pltpu.make_async_copy(out.at[g], fetched.at[g, :, own], local)
    first.start()
    half = n_exp // 2
    order = []
    for k in range(half):
        order.append(half + k)
        if k:
            order.append(k)
    sends = {}
    for k in order:
        e = flip(g, k)
        sends[k] = remote(out.at[e], fetched.at[g, :, own], s0.at[k], r0.at[k], (e, s))
        sends[k].start()
    crossed, done = [], []
    for k in range(n_exp):
        block = fetched.at[flip(g, k)]
        if k:
            sends[k].wait_recv()
        else:
            first.wait()
        c = remote(block.at[:, own], block.at[:, own], sa.at[k], ra.at[k], across)
        c.start()
        crossed.append(c)
        d = remote(block.at[:, own], block.at[:, own], sb.at[k], rb.at[k], beside)
        d.start()
        done.append(d)
    for k in range(n_exp):
        block = fetched.at[flip(g, k)]
        crossed[k].wait_recv()
        d = remote(block.at[:, theirs], block.at[:, theirs], sc.at[k], rc.at[k], beside)
        d.start()
        done.append(d)
    for k in order:
        sends[k].wait_send()
    for c in crossed:
        c.wait_send()
    for d in done:
        d.wait()


def dispatch(n_exp, n_seq, out):
    rows, width = out.shape[1:]
    dma = pltpu.SemaphoreType.DMA
    return pl.pallas_call(
        functools.partial(dispatch_kernel, n_exp),
        out_shape=jax.ShapeDtypeStruct((n_exp, rows, n_seq * width), out.dtype),
        in_specs=[ANY],
        out_specs=ANY,
        scratch_shapes=[dma((n_exp,))] * 8 + [dma],
        compiler_params=pltpu.CompilerParams(collective_id=1, has_side_effects=True),
    )(out)


def combine_kernel(n_exp, part, arrived, near, sum1, far, sum2, s1, r1, s2, r2, s3, r3, local):
    g, s = lax.axis_index("exp"), lax.axis_index("seq")
    width = arrived.shape[2]
    across, beside = (g, flip(s, 2)), (g, flip(s, 1))
    own, theirs = columns(s, width), columns(flip(s, 2), width)
    greet([(flip(g, k), s) for k in range(1, n_exp)] + [across, beside])
    half = n_exp // 2
    order = list(range(half, n_exp)) + list(range(1, half)) + [0]
    pairs = {}
    for k in order:
        e = flip(g, k)
        pairs[k] = [
            remote(
                part.at[e, :, columns(flip(s, bits), width)],
                near.at[e, i],
                s1.at[k, i],
                r1.at[k, i],
                beside,
            )
            for i, bits in enumerate((3, 1))
        ]
        for c in pairs[k]:
            c.start()
    middle, last = {}, {}
    for k in order:
        e = flip(g, k)
        pairs[k][0].wait_recv()
        both = part[e, :, theirs].astype(jnp.float32) + near[e, 0].astype(jnp.float32)
        sum1[e] = both.astype(jnp.bfloat16)
        middle[k] = remote(sum1.at[e], far.at[e], s2.at[k], r2.at[k], across)
        middle[k].start()
    for k in order:
        e = flip(g, k)
        pairs[k][1].wait_recv()
        middle[k].wait_recv()
        total = part[e, :, own].astype(jnp.float32) + near[e, 1].astype(jnp.float32)
        total = total + far[e].astype(jnp.float32)
        sum2[e] = total.astype(jnp.bfloat16)
        if k:
            last[k] = remote(sum2.at[e], arrived.at[g], s3.at[k], r3.at[k], (e, s))
        else:
            last[k] = pltpu.make_async_copy(sum2.at[e], arrived.at[g], local)
        last[k].start()
    for k in order:
        for c in pairs[k]:
            c.wait_send()
        middle[k].wait_send()
        last[k].wait()


def combine(n_exp, n_seq, part):
    rows, width = part.shape[1], part.shape[2] // n_seq
    dma = pltpu.SemaphoreType.DMA
    block = pltpu.VMEM((n_exp, rows, width), part.dtype)
    return pl.pallas_call(
        functools.partial(combine_kernel, n_exp),
        out_shape=jax.ShapeDtypeStruct((n_exp, rows, width), part.dtype),
        in_specs=[VMEM],
        out_specs=VMEM,
        scratch_shapes=[pltpu.VMEM((n_exp, 2, rows, width), part.dtype), block, block, block]
        + [dma((n_exp, 2))] * 2
        + [dma((n_exp,))] * 4
        + [dma],
        compiler_params=pltpu.CompilerParams(
            collective_id=2, has_side_effects=True, vmem_limit_bytes=48 * 2**20
        ),
    )(part)


def regroup_kernel(n_seq, totals, out, send, recv, local):
    g, s = lax.axis_index("exp"), lax.axis_index("seq")
    width = totals.shape[2]
    own = columns(s, width)
    greet([(g, flip(s, k)) for k in range(1, n_seq)])
    copies = []
    for k in range(n_seq - 1, 0, -1):
        t = flip(s, k)
        copies.append(remote(totals.at[t], out.at[:, own], send.at[k], recv.at[k], (g, t)))
        copies[-1].start()
    mine = pltpu.make_async_copy(totals.at[s], out.at[:, own], local)
    mine.start()
    for c in copies:
        c.wait()
    mine.wait()


def regroup(n_seq, totals):
    rows, width = totals.shape[1:]
    dma = pltpu.SemaphoreType.DMA
    return pl.pallas_call(
        functools.partial(regroup_kernel, n_seq),
        out_shape=jax.ShapeDtypeStruct((rows, n_seq * width), totals.dtype),
        in_specs=[VMEM],
        out_specs=VMEM,
        scratch_shapes=[dma((n_seq,)), dma((n_seq,)), dma],
        compiler_params=pltpu.CompilerParams(collective_id=3, has_side_effects=True),
    )(totals)


def local(out_grad, chosen, scores, saved_pre, gate_up, down):
    n_exp = lax.axis_size("exp")
    n_seq = lax.axis_size("seq")
    capacity = chosen.shape[1]
    slot_most = 9 * capacity // (8 * n_exp)
    tok_count, model_width = out_grad.shape
    width = model_width // n_seq
    group_tok = tok_count * n_seq
    pad_rows = n_exp * slot_most
    hidden_part = gate_up.shape[3]
    group_index = lax.axis_index("exp")

    own_ids = chosen[0]
    owner_group = own_ids // group_tok
    owner_hits = (owner_group[None, :] == jnp.arange(n_exp, dtype=jnp.int32)[:, None]).astype(
        jnp.int32
    )
    slot_order = jnp.sum(jnp.cumsum(owner_hits, axis=1) * owner_hits, axis=0) - 1
    position = owner_group * slot_most + slot_order
    place = position[None, :] == jnp.arange(pad_rows, dtype=jnp.int32)[:, None]
    weight_padded = jnp.sum(jnp.where(place, scores[0][None, :], 0.0), axis=1)
    place_one = place.astype(jnp.bfloat16)

    def padded(x):
        return jnp.dot(place_one, x, preferred_element_type=jnp.float32)

    gate_pre = padded(saved_pre[0, :, 0])
    up_pre = padded(saved_pre[0, :, 1])
    mixing = gate_up[0].reshape(model_width, 2 * hidden_part)

    ids, group = exchange(n_exp, n_seq, chosen.reshape(capacity // 128, 128), out_grad)
    local_ids = ids.reshape(n_exp, capacity) - group_index * group_tok
    inside = (local_ids >= 0) & (local_ids < group_tok)
    slot_rank = jnp.cumsum(inside.astype(jnp.int32), axis=1) - 1
    slot_ids = jnp.arange(slot_most, dtype=jnp.int32)
    picked = inside[:, None, :] & (slot_rank[:, None, :] == slot_ids[None, :, None])
    source = jnp.sum(jnp.where(picked, local_ids[:, None, :] + 1, 0), axis=2).reshape(pad_rows) - 1
    tokens = jnp.arange(group_tok, dtype=jnp.int32)
    take = (source[:, None] == tokens[None, :]).astype(jnp.bfloat16)
    outgoing = jnp.dot(
        take, group.reshape(group_tok, width), preferred_element_type=jnp.float32
    ).astype(jnp.bfloat16)
    fetched = dispatch(n_exp, n_seq, outgoing.reshape(n_exp, slot_most, width))
    fetched = fetched.reshape(pad_rows, model_width)

    back_grad = lax.dot_general(
        fetched, down[0], (((1,), (1,)), ((), ())), preferred_element_type=jnp.float32
    )
    sigmoid_gate = jax.nn.sigmoid(gate_pre)
    activated = gate_pre * sigmoid_gate
    hidden = (activated * up_pre).astype(jnp.bfloat16)
    hidden = lax.optimization_barrier(hidden)
    score_part = jnp.sum(hidden.astype(jnp.float32) * back_grad, axis=1)
    scaled = weight_padded[:, None] * back_grad
    d_gate = scaled * up_pre * sigmoid_gate * (1.0 + gate_pre * (1.0 - sigmoid_gate))
    d_up = scaled * activated
    d_both = jnp.concatenate([d_gate, d_up], axis=1).astype(jnp.bfloat16)
    partial_value = lax.dot_general(
        d_both, mixing, (((1,), (1,)), ((), ())), preferred_element_type=jnp.float32
    ).astype(jnp.bfloat16)
    score_slots = jnp.sum(jnp.where(place, score_part[:, None], 0.0), axis=0)
    score_grad = lax.psum(score_slots, "seq")[None, :]

    arrived = combine(n_exp, n_seq, partial_value.reshape(n_exp, slot_most, model_width))
    totals = lax.dot_general(
        take,
        arrived.reshape(pad_rows, width),
        (((0,), (0,)), ((), ())),
        preferred_element_type=jnp.float32,
    ).astype(jnp.bfloat16)
    summed = regroup(n_seq, totals.reshape(n_seq, tok_count, width))
    return (summed, score_grad)


def solution(mesh):
    return jax.shard_map(
        local,
        mesh=mesh,
        in_specs=(
            P(("exp", "seq"), None),
            P("exp", None),
            P("exp", None),
            P("exp", None, None, "seq"),
            P("exp", None, None, "seq"),
            P("exp", "seq", None),
        ),
        out_specs=(P(("exp", "seq"), None), P("exp", None)),
        check_vma=False,
    )
```

time: 617 us -> 235 us (0.38)
  blocking collectives: 246 us -> 6.35 us
  Pallas kernels: 0 us -> 181 us
  local copies, waits for them, and re-layouts: 168 us -> 9.67 us
  waiting for transfers between devices: 93.4 us -> 0 us
  other arithmetic: 63.5 us -> 9.95 us
  between operations: 14.2 us -> 0.87 us
  starting transfers between devices: 6.22 us -> 0 us
    all_to_all x1 -> x0, blocking collectives: 211 us -> none  [local(): lax.all_to_all(partial_value, 'exp', split_axis=0, concat_axis=0, tiled=T...]
    pallas_call x0 -> x4, Pallas kernels: none -> 181 us  [the longest x1 76.3 us: dispatch(): pl.pallas_call(functools.partial(dispatch_kernel, n_exp), out_shape=jax.S...]
    scatter x2 -> x0, local copies, waits for them, and re-layouts: 115 us -> none  [the longest x1 110 us: local(): jnp.zeros((pad_rows, 2, hidden_part), jnp.bfloat16).at[position]]
    all_to_all x1 -> x0, waiting for transfers between devices: 58 us -> none  [local(): lax.all_to_all(outgoing, 'exp', split_axis=0, concat_axis=0, tiled=True)]
    scatter-add x1 -> x0, other arithmetic: 39.5 us -> none  [local(): totals = jnp.zeros((group_tok, model_width), jnp.float32).at[source_row]....]
    reduce_scatter x1 -> x0, waiting for transfers between devices: 30.4 us -> none  [local(): lax.psum_scatter(totals.astype(jnp.bfloat16), 'seq', scatter_dimension=0,...]
    all_gather x1 -> x0, blocking collectives: 28.2 us -> none  [local(): all_ids = lax.all_gather(chosen, 'exp', axis=0, tiled=True)]
    gather x2 -> x0, local copies, waits for them, and re-layouts: 27.3 us -> none  [the longest x1 21.1 us: local(): group_grad[source_row]]
  transfers between devices with their start and end apart: 3 -> 0, of which waited for: 3 -> 0; matrix products, arithmetic and copies ran while one was open for 26% -> 0% of each run, Pallas kernels for 0% -> 0%
where the time goes in v1:
time: 235 us; the launch traced here: 232 us
  Pallas kernels  181 us (77%)
  matrix products  24.1 us (10%)
  other arithmetic  9.95 us (4%)
  local copies, waits for them, and re-layouts  9.67 us (4%)
  blocking collectives  6.35 us (3%)
    pallas_call x1, Pallas kernels, dispatch(): pl.pallas_call(functools.partial(dispatch_kernel, n_exp), out_shape=jax.S...  76.3 us
    pallas_call x1, Pallas kernels, combine(): pl.pallas_call(functools.partial(combine_kernel, n_exp), out_shape=jax.Sh...  68.7 us
    pallas_call x1, Pallas kernels, exchange(): pl.pallas_call(functools.partial(exchange_kernel, n_exp, n_seq), out_shap...  19.3 us
    pallas_call x1, Pallas kernels, regroup(): pl.pallas_call(functools.partial(regroup_kernel, n_seq), out_shape=jax.Sh...  16.6 us
    dot_general x1, matrix products, local(): lax.dot_general(d_both, mixing, (((1,), (1,)), ((), ())), preferred_eleme...  10.1 us
    psum x1, blocking collectives, local(): score_grad = lax.psum(score_slots, 'seq')[None, :]  6.35 us
    another operation x5, other arithmetic  5.86 us

profile of v1, /device:TPU:8, one launch (start us, length us, event | category | flops | bytes accessed | tf_op | source)
XLA Modules:
  0.0 231.8 jit_solution(3542965358762578076)
XLA Ops:
  0.6 19.3 %shard_map.77 = (s32[8,8,128]{2,1,0:T(8,128)}, bf16[4,128,1024]{2,1,0:T(8,128)(2,1)}) custom-call(s32[8,128]{1,0:T(8,128)} %bitcast.57, bf16[128,4096]{1,0:T(8,128)(2,1)} %grad.1), custom_call_target="tpu_custom_call" | custom-call | tf_op jit(solution)/shard_map/pallas_call | solution.py:68
  20.0 0.8 fusion.17
  20.8 2.3 reduce-window.14
  23.0 0.3 slice_reduce_fusion.1
  23.6 0.8 add_bitcast_fusion
  24.4 1.1 select_reduce_fusion.2
  25.5 4.1 %convolution_convert_fusion.1 = bf16[1152,1024]{1,0:T(8,128)(2,1)} fusion(bf16[512,1024]{1,0:T(8,128)(2,1)} %bitcast.70, s32[1152]{0:T(1024)S(1)} %sub.47), kind=kOutput, calls=%fused_computation.9 | convolution fusion | flops 1209729024 | bytes 3412480 | tf_op jit(solution)/shard_map/dot_general | solution.py:278
  29.6 76.3 %shard_map.78 = bf16[8,144,4096]{2,1,0:T(8,128)(2,1)} custom-call(bf16[8,144,1024]{2,1,0:T(8,128)(2,1)} %bitcast.55), custom_call_target="tpu_custom_call" | custom-call | tf_op jit(solution)/shard_map/pallas_call | solution.py:130
  106.0 2.3 reduce-window.16
  108.8 4.6 %fusion.18 = (bf16[1,1024,1,384]{3,2,1,0:T(2,128)(2,1)S(1)}, bf16[1,1024,1,384]{3,2,1,0:T(2,128)(2,1)S(1)}) fusion(bf16[1,1024,2,384]{3,2,1,0:T(2,128)(2,1)} %param.9), kind=kLoop, calls=%fused_computation.50 | loop fusion | bytes 3145728 | tf_op jit(solution)/shard_map/slice | solution.py:265
  113.4 1.3 fusion
  114.8 1.5 multiply_convert_fusion
  116.4 0.5 slice-done.1
  116.9 0.4 slice-done.2
  117.3 4.5 %multiply_reduce_fusion = (f32[1152]{0:T(1024)S(1)}, f32[1152,384]{0,1:T(8,128)S(1)}) fusion(bf16[1152,384]{0,1:T(8,128)(2,1)S(1)} %get-tuple-element.14, bf16[1152,4096]{1,0:T(8,128)(2,1)S(1)} %bitcast.49, bf16[1,384,4096]{2,1,0:T(8,128)(2,1)S(1)} %copy-done), kind=kOutput, calls=%fused_computation.19 | convolution fusion | flops 3625204736 | bytes 15241728 | tf_op jit(solution)/shard_map/dot_general | solution.py:284
  121.8 1.2 select_reduce_fusion
  123.0 1.0 multiply_convert_fusion.2
  124.1 1.2 copy.17
  125.2 10.1 %convolution_convert_fusion = bf16[1152,4096]{1,0:T(8,128)(2,1)} fusion(bf16[4096,768]{1,0:T(8,128)(2,1)S(1)} %bitcast.54, bf16[1152,384]{0,1:T(8,128)(2,1)S(1)} %get-tuple-element.11, bf16[1152,384]{0,1:T(8,128)(2,1)S(1)} %get-tuple-element.10), kind=kOutput, calls=%fused_computation | convolution fusion | flops 7256014848 | bytes 17498112 | tf_op jit(solution)/shard_map/dot_general | solution.py:296
  135.3 68.7 %shard_map.79 = bf16[8,144,1024]{2,1,0:T(8,128)(2,1)S(1)} custom-call(bf16[8,144,4096]{2,1,0:T(8,128)(2,1)} %bitcast.50), custom_call_target="tpu_custom_call" | custom-call | tf_op jit(solution)/shard_map/pallas_call | solution.py:194
  204.0 2.6 %fusion.12 = bf16[512,1024]{1,0:T(8,128)(2,1)} fusion(bf16[1152,1024]{1,0:T(8,128)(2,1)S(1)} %bitcast.46, s32[1152]{0:T(1024)S(1)} %sub.47), kind=kOutput, calls=%fused_computation.25 | convolution fusion | flops 1209073664 | bytes 3412480 | tf_op jit(solution)/shard_map/dot_general | solution.py:303
  206.6 16.6 %shard_map.80 = bf16[128,4096]{1,0:T(8,128)(2,1)} custom-call(bf16[4,128,1024]{2,1,0:T(8,128)(2,1)} %bitcast.56), custom_call_target="tpu_custom_call" | custom-call | tf_op jit(solution)/shard_map/pallas_call | solution.py:229
  223.2 6.4 %psum.7 = f32[1,1024]{1,0:T(1,128)} all-reduce(f32[1,1024]{1,0:T(1,128)S(1)} %bitcast.65), channel_id=1, replica_groups=mesh['exp'=8,'seq'=4] {'seq'}, use_global_device_ids=true, to_apply=%region_9.10 | all-reduce | flops 1024 | bytes 8192 | tf_op jit(solution)/shard_map/psum | solution.py:300
  229.5 2.3 copy.29
  (29 shorter events, 1.0 us)
Async XLA Ops:
  0.6 115.7 %copy-start = (bf16[1,384,4096]{2,1,0:T(8,128)(2,1)S(1)}, bf16[1,384,4096]{2,1,0:T(8,128)(2,1)}, u32[]{:S(2)}) copy-start(bf16[1,384,4096]{2,1,0:T(8,128)(2,1)} %param.11) | copy-start | bytes 9437188
  29.6 76.3 %copy-start.1 = (s32[1,1024]{1,0:T(1,128)S(1)}, s32[1,1024]{1,0:T(1,128)}, u32[]{:S(2)}) copy-start(s32[1,1024]{1,0:T(1,128)} %param.7) | copy-start | bytes 12292
  113.4 3.0 %slice-start = ((s8[9437184]{0:T(1024)(128)(4,1)}), s8[4194304]{0:T(1024)(128)(4,1)S(1)}, s32[]{:S(2)}) async-start(s8[9437184]{0:T(1024)(128)(4,1)} %bitcast.47), calls=%async_computation | async-start | bytes 8388608
  113.4 3.5 %slice-start.1 = ((s8[9437184]{0:T(1024)(128)(4,1)}), s8[4194304]{0:T(1024)(128)(4,1)S(1)}, s32[]{:S(2)}) async-start(s8[9437184]{0:T(1024)(128)(4,1)} %bitcast.47), calls=%async_computation.1 | async-start | bytes 8388608
  114.8 2.5 %slice-start.2 = ((s8[9437184]{0:T(1024)(128)(4,1)}), s8[1048576]{0:T(1024)(128)(4,1)S(1)}, s32[]{:S(2)}) async-start(s8[9437184]{0:T(1024)(128)(4,1)} %bitcast.47), calls=%async_computation.2 | async-start | bytes 2097152
  114.8 9.2 %slice-start.3 = ((s8[6291456]{0:T(1024)(128)(4,1)}), s8[4194304]{0:T(1024)(128)(4,1)S(1)}, s32[]{:S(2)}) async-start(s8[6291456]{0:T(1024)(128)(4,1)} %bitcast.51), calls=%async_computation.3 | async-start | bytes 8388608
  117.3 4.5 %copy-start.2 = (f32[1,1024]{1,0:T(1,128)S(1)}, f32[1,1024]{1,0:T(1,128)}, u32[]{:S(2)}) copy-start(f32[1,1024]{1,0:T(1,128)} %param.8) | copy-start | bytes 12292
  117.3 6.7 %slice-start.4 = ((s8[6291456]{0:T(1024)(128)(4,1)}), s8[2097152]{0:T(1024)(128)(4,1)S(1)}, s32[]{:S(2)}) async-start(s8[6291456]{0:T(1024)(128)(4,1)} %bitcast.51), calls=%async_computation.4 | async-start | bytes 4194304

commit v2 on v1

--- a/solution.py
+++ b/solution.py
@@ -206,7 +206,173 @@
     )(part)
 
 
-def regroup_kernel(n_seq, totals, out, send, recv, local):
+def expert_kernel(
+    n_exp, out, gate, up, weight, down, mixing, arrived, score,
+    fetched, both, part, near, sum1, far, sum2,
+    s0, r0, sa, ra, sb, rb, sc, rc, s1, r1, s2, r2, s3, r3, local,
+):
+    g, s = lax.axis_index("exp"), lax.axis_index("seq")
+    width = out.shape[2]
+    hidden_part = gate.shape[2]
+    across, beside = (g, flip(s, 2)), (g, flip(s, 1))
+    own, theirs = columns(s, width), columns(flip(s, 2), width)
+    greet([(flip(g, k), s) for k in range(1, n_exp)] + [across, beside])
+    half = n_exp // 2
+    place = [flip(g, k) for k in range(n_exp)]
+    first = pltpu.make_async_copy(out.at[g], fetched.at[g, :, own], local.at[0])
+    first.start()
+    sends, crossed, moved, turned, pairs, middle, last = {}, {}, {}, {}, {}, {}, {}
+
+    def send(k):
+        sends[k] = remote(
+            out.at[place[k]], fetched.at[g, :, own], s0.at[k], r0.at[k], (place[k], s)
+        )
+        sends[k].start()
+
+    def spread(k):
+        block = fetched.at[place[k], :, own]
+        if k:
+            sends[k].wait_recv()
+        else:
+            first.wait()
+        crossed[k] = remote(block, block, sa.at[k], ra.at[k], across)
+        crossed[k].start()
+        moved[k] = remote(block, block, sb.at[k], rb.at[k], beside)
+        moved[k].start()
+
+    def turn(k):
+        block = fetched.at[place[k], :, theirs]
+        crossed[k].wait_recv()
+        turned[k] = remote(block, block, sc.at[k], rc.at[k], beside)
+        turned[k].start()
+
+    def compute(k):
+        e = place[k]
+        moved[k].wait_recv()
+        turned[k].wait_recv()
+        back = lax.dot_general(
+            fetched[e], down[...], (((1,), (1,)), ((), ())), preferred_element_type=jnp.float32
+        )
+        gate_pre = gate[e].astype(jnp.float32)
+        up_pre = up[e].astype(jnp.float32)
+        sigmoid_gate = jax.nn.sigmoid(gate_pre)
+        activated = gate_pre * sigmoid_gate
+        hidden = (activated * up_pre).astype(jnp.bfloat16)
+        score[e] = jnp.sum(hidden.astype(jnp.float32) * back, axis=1, keepdims=True)
+        scaled = weight[e] * back
+        d_gate = scaled * up_pre * sigmoid_gate * (1.0 + gate_pre * (1.0 - sigmoid_gate))
+        both[:, :hidden_part] = d_gate.astype(jnp.bfloat16)
+        both[:, hidden_part:] = (scaled * activated).astype(jnp.bfloat16)
+
+        @pl.loop(0, mixing.shape[0] // 512)
+        def _(i):
+            tile = columns(i, 512)
+            part[e, :, tile] = lax.dot_general(
+                both[...],
+                mixing[tile, :],
+                (((1,), (1,)), ((), ())),
+                preferred_element_type=jnp.float32,
+            ).astype(jnp.bfloat16)
+
+        pairs[k] = [
+            remote(
+                part.at[e, :, columns(flip(s, bits), width)],
+                near.at[e, i],
+                s1.at[k, i],
+                r1.at[k, i],
+                beside,
+            )
+            for i, bits in enumerate((3, 1))
+        ]
+        for c in pairs[k]:
+            c.start()
+
+    def hand(k):
+        e = place[k]
+        pairs[k][0].wait_recv()
+        value = part[e, :, theirs].astype(jnp.float32) + near[e, 0].astype(jnp.float32)
+        sum1[e] = value.astype(jnp.bfloat16)
+        middle[k] = remote(sum1.at[e], far.at[e], s2.at[k], r2.at[k], across)
+        middle[k].start()
+
+    def give(k):
+        e = place[k]
+        pairs[k][1].wait_recv()
+        middle[k].wait_recv()
+        value = part[e, :, own].astype(jnp.float32) + near[e, 1].astype(jnp.float32)
+        value = value + far[e].astype(jnp.float32)
+        sum2[e] = value.astype(jnp.bfloat16)
+        if k:
+            last[k] = remote(sum2.at[e], arrived.at[g], s3.at[k], r3.at[k], (e, s))
+        else:
+            last[k] = pltpu.make_async_copy(sum2.at[e], arrived.at[g], local.at[1])
+        last[k].start()
+
+    batches = [list(range(half))] + [list(range(k, k + 2)) for k in range(half, n_exp, 2)]
+    for k in batches[1]:
+        send(k)
+    for k in batches[0][1:]:
+        send(k)
+    previous = []
+    for i, batch in enumerate(batches):
+        for k in batch:
+            spread(k)
+        if 0 < i < len(batches) - 1:
+            for k in batches[i + 1]:
+                send(k)
+        for k in previous:
+            give(k)
+        for k in batch:
+            turn(k)
+        for j, k in enumerate(batch):
+            compute(k)
+            if j:
+                hand(batch[j - 1])
+        hand(batch[-1])
+        previous = batch
+    for k in previous:
+        give(k)
+    for k in range(n_exp):
+        if k:
+            sends[k].wait_send()
+        crossed[k].wait_send()
+        moved[k].wait_send()
+        turned[k].wait_send()
+        for c in pairs[k]:
+            c.wait_send()
+        middle[k].wait_send()
+        last[k].wait()
+
+
+def expert(n_exp, n_seq, out, gate, up, weight, down, mixing):
+    rows, width = out.shape[1:]
+    model_width = n_seq * width
+    dma = pltpu.SemaphoreType.DMA
+    block = pltpu.VMEM((n_exp, rows, width), out.dtype)
+    whole = pltpu.VMEM((n_exp, rows, model_width), out.dtype)
+    return pl.pallas_call(
+        functools.partial(expert_kernel, n_exp),
+        out_shape=(
+            jax.ShapeDtypeStruct((n_exp, rows, width), out.dtype),
+            jax.ShapeDtypeStruct((n_exp, rows, 1), jnp.float32),
+        ),
+        in_specs=[VMEM] * 6,
+        out_specs=(VMEM, VMEM),
+        scratch_shapes=[whole, pltpu.VMEM((rows, mixing.shape[1]), out.dtype), whole]
+        + [pltpu.VMEM((n_exp, 2, rows, width), out.dtype), block, block, block]
+        + [dma((n_exp,))] * 8
+        + [dma((n_exp, 2))] * 2
+        + [dma((n_exp,))] * 4
+        + [dma((2,))],
+        compiler_params=pltpu.CompilerParams(
+            collective_id=4, has_side_effects=True, vmem_limit_bytes=58 * 2**20
+        ),
+    )(out, gate, up, weight, down, mixing)
+
+
+def regroup_kernel(
+    n_seq, totals, score, out, score_sum, scores, send, recv, send_s, recv_s, local
+):
     g, s = lax.axis_index("exp"), lax.axis_index("seq")
     width = totals.shape[2]
     own = columns(s, width)
@@ -216,24 +382,36 @@
         t = flip(s, k)
         copies.append(remote(totals.at[t], out.at[:, own], send.at[k], recv.at[k], (g, t)))
         copies[-1].start()
+        copies.append(remote(score, scores.at[s], send_s.at[k], recv_s.at[k], (g, t)))
+        copies[-1].start()
     mine = pltpu.make_async_copy(totals.at[s], out.at[:, own], local)
     mine.start()
+    scores[s] = score[...]
     for c in copies:
         c.wait()
+    value = scores[0]
+    for k in range(1, n_seq):
+        value = value + scores[k]
+    score_sum[...] = value
     mine.wait()
 
 
-def regroup(n_seq, totals):
+def regroup(n_seq, totals, score):
     rows, width = totals.shape[1:]
     dma = pltpu.SemaphoreType.DMA
     return pl.pallas_call(
         functools.partial(regroup_kernel, n_seq),
-        out_shape=jax.ShapeDtypeStruct((rows, n_seq * width), totals.dtype),
-        in_specs=[VMEM],
-        out_specs=VMEM,
-        scratch_shapes=[dma((n_seq,)), dma((n_seq,)), dma],
+        out_shape=(
+            jax.ShapeDtypeStruct((rows, n_seq * width), totals.dtype),
+            jax.ShapeDtypeStruct(score.shape, score.dtype),
+        ),
+        in_specs=[VMEM, VMEM],
+        out_specs=(VMEM, VMEM),
+        scratch_shapes=[pltpu.VMEM((n_seq,) + score.shape, score.dtype)]
+        + [dma((n_seq,))] * 4
+        + [dma],
         compiler_params=pltpu.CompilerParams(collective_id=3, has_side_effects=True),
-    )(totals)
+    )(totals, score)
 
 
 def local(out_grad, chosen, scores, saved_pre, gate_up, down):
@@ -278,36 +456,52 @@
     outgoing = jnp.dot(
         take, group.reshape(group_tok, width), preferred_element_type=jnp.float32
     ).astype(jnp.bfloat16)
-    fetched = dispatch(n_exp, n_seq, outgoing.reshape(n_exp, slot_most, width))
-    fetched = fetched.reshape(pad_rows, model_width)
-
-    back_grad = lax.dot_general(
-        fetched, down[0], (((1,), (1,)), ((), ())), preferred_element_type=jnp.float32
-    )
-    sigmoid_gate = jax.nn.sigmoid(gate_pre)
-    activated = gate_pre * sigmoid_gate
-    hidden = (activated * up_pre).astype(jnp.bfloat16)
-    hidden = lax.optimization_barrier(hidden)
-    score_part = jnp.sum(hidden.astype(jnp.float32) * back_grad, axis=1)
-    scaled = weight_padded[:, None] * back_grad
-    d_gate = scaled * up_pre * sigmoid_gate * (1.0 + gate_pre * (1.0 - sigmoid_gate))
-    d_up = scaled * activated
-    d_both = jnp.concatenate([d_gate, d_up], axis=1).astype(jnp.bfloat16)
-    partial_value = lax.dot_general(
-        d_both, mixing, (((1,), (1,)), ((), ())), preferred_element_type=jnp.float32
-    ).astype(jnp.bfloat16)
+    outgoing = outgoing.reshape(n_exp, slot_most, width)
+    if slot_most % 16 == 0:
+        arrived, score_part = expert(
+            n_exp,
+            n_seq,
+            outgoing,
+            gate_pre.astype(jnp.bfloat16).reshape(n_exp, slot_most, hidden_part),
+            up_pre.astype(jnp.bfloat16).reshape(n_exp, slot_most, hidden_part),
+            weight_padded.reshape(n_exp, slot_most, 1),
+            down[0],
+            mixing,
+        )
+        score_part = score_part.reshape(pad_rows)
+    else:
+        fetched = dispatch(n_exp, n_seq, outgoing)
+        fetched = fetched.reshape(pad_rows, model_width)
+
+        back_grad = lax.dot_general(
+            fetched, down[0], (((1,), (1,)), ((), ())), preferred_element_type=jnp.float32
+        )
+        sigmoid_gate = jax.nn.sigmoid(gate_pre)
+        activated = gate_pre * sigmoid_gate
+        hidden = (activated * up_pre).astype(jnp.bfloat16)
+        hidden = lax.optimization_barrier(hidden)
+        score_part = jnp.sum(hidden.astype(jnp.float32) * back_grad, axis=1)
+        scaled = weight_padded[:, None] * back_grad
+        d_gate = scaled * up_pre * sigmoid_gate * (1.0 + gate_pre * (1.0 - sigmoid_gate))
+        d_up = scaled * activated
+        d_both = jnp.concatenate([d_gate, d_up], axis=1).astype(jnp.bfloat16)
+        partial_value = lax.dot_general(
+            d_both, mixing, (((1,), (1,)), ((), ())), preferred_element_type=jnp.float32
+        ).astype(jnp.bfloat16)
+        arrived = combine(n_exp, n_seq, partial_value.reshape(n_exp, slot_most, model_width))
     score_slots = jnp.sum(jnp.where(place, score_part[:, None], 0.0), axis=0)
-    score_grad = lax.psum(score_slots, "seq")[None, :]
-
-    arrived = combine(n_exp, n_seq, partial_value.reshape(n_exp, slot_most, model_width))
     totals = lax.dot_general(
         take,
         arrived.reshape(pad_rows, width),
         (((0,), (0,)), ((), ())),
         preferred_element_type=jnp.float32,
     ).astype(jnp.bfloat16)
-    summed = regroup(n_seq, totals.reshape(n_seq, tok_count, width))
-    return (summed, score_grad)
+    summed, score_grad = regroup(
+        n_seq,
+        totals.reshape(n_seq, tok_count, width),
+        score_slots.reshape(capacity // 128, 128),
+    )
+    return (summed, score_grad.reshape(1, capacity))
 
 
 def solution(mesh):

time: 235 us -> 235 us (level); the launches traced: 232 us -> 234 us
  Pallas kernels: 181 us -> 197 us
  matrix products: 24.1 us -> 13.2 us
  blocking collectives: 6.35 us -> 0 us
    pallas_call x3 -> x2, Pallas kernels: 162 us -> 178 us  [the longest x1 161 us: expert(): pl.pallas_call(functools.partial(expert_kernel, n_exp), out_shape=(jax.Sh...]
    dot_general x2 -> x0, matrix products: 14.5 us -> none  [the longest x1 10.1 us: local(): lax.dot_general(d_both, mixing, (((1,), (1,)), ((), ())), preferred_eleme...]
    psum x1 -> x0, blocking collectives: 6.35 us -> none  [local(): score_grad = lax.psum(score_slots, 'seq')[None, :]]
    unnamed x19 -> x12, local copies, waits for them, and re-layouts: 4.41 us -> 7.41 us
    slice x2, local copies, waits for them, and re-layouts: 4.88 us -> 2.49 us  [the longest x1 2.22 us: local(): up_pre = padded(saved_pre[0, :, 1])]
    another operation x5 -> x4, other arithmetic: 5.86 us -> 4.86 us
where the time goes in v2:
time: 235 us; the launch traced here: 234 us
  Pallas kernels  197 us (84%)
  matrix products  13.2 us (6%)
  other arithmetic  11.8 us (5%)
  local copies, waits for them, and re-layouts  11.6 us (5%)
    pallas_call x1, Pallas kernels, expert(): pl.pallas_call(functools.partial(expert_kernel, n_exp), out_shape=(jax.Sh...  161 us
    pallas_call x1, Pallas kernels, exchange(): pl.pallas_call(functools.partial(exchange_kernel, n_exp, n_seq), out_shap...  19.2 us
    pallas_call x1, Pallas kernels, regroup(): pl.pallas_call(functools.partial(regroup_kernel, n_seq), out_shape=(jax.S...  16.8 us
    unnamed x12, local copies, waits for them, and re-layouts  7.41 us
    another operation x4, other arithmetic  4.86 us

profile of v2, /device:TPU:8, one launch (start us, length us, event | category | flops | bytes accessed | tf_op | source)
XLA Modules:
  0.0 234.4 jit_solution(11360520953242600522)
XLA Ops:
  0.6 0.7 and_select_fusion
  1.4 2.3 reduce-window.16
  3.6 0.3 slice_reduce_fusion
  4.2 0.7 multiply_add_fusion
  4.9 1.2 select_reduce_fusion.1
  6.1 1.3 reshape.139.weight
  7.4 19.2 %shard_map.77 = (s32[8,8,128]{2,1,0:T(8,128)}, bf16[4,128,1024]{2,1,0:T(8,128)(2,1)}) custom-call(s32[8,128]{1,0:T(8,128)} %bitcast.48, bf16[128,4096]{1,0:T(8,128)(2,1)} %grad.1), custom_call_target="tpu_custom_call" | custom-call | tf_op jit(solution)/shard_map/pallas_call | solution.py:68
  26.6 0.8 add_bitcast_fusion
  27.3 0.8 fusion.12
  28.1 2.3 reduce-window.14
  30.4 0.3 slice_reduce_fusion.1
  30.9 1.1 select_reduce_fusion.2
  32.1 4.2 %convolution_convert_fusion = bf16[1152,1024]{1,0:T(8,128)(2,1)} fusion(bf16[512,1024]{1,0:T(8,128)(2,1)} %bitcast.64, s32[1152]{0:T(1024)S(1)} %sub.44), kind=kOutput, calls=%fused_computation.8 | convolution fusion | flops 1209729024 | bytes 3412480 | tf_op jit(solution)/shard_map/dot_general | solution.py:456
  36.3 2.2 fusion.13
  38.6 2.3 fusion.4
  40.9 2.3 fusion.3
  43.2 3.8 %copy.19 = bf16[512,8,2,384]{3,1,2,0:T(8,128)(2,1)} copy(bf16[512,8,2,384]{3,2,1,0:T(2,128)(2,1)S(1)} %bitcast.42) | data formatting | bytes 12582912
  47.0 161.0 %shard_map.78 = (bf16[8,144,1024]{2,1,0:T(8,128)(2,1)}, f32[8,144,1]{2,1,0:T(8,128)}) custom-call(bf16[8,144,1024]{2,1,0:T(8,128)(2,1)} %bitcast.44, bf16[8,144,384]{2,1,0:T(8,128)(2,1)} %bitcast.47, bf16[8,144,384]{2,1,0:T(8,128)(2,1)} %bitcast.46, f32[8,144,1]{2,1,0:T(8,128)} %reshape.139.weight, bf16[384,4096]{1,0:T(8,128)(2,1)} %bitcast.43, ...), custom_call_target="tpu_custom_call" | custom-call | tf_op jit(solution)/shard_map/pallas_call | solution.py:353
  208.0 4.3 %fusion.8 = bf16[512,1024]{1,0:T(8,128)(2,1)} fusion(bf16[1152,1024]{1,0:T(8,128)(2,1)} %bitcast.63, s32[1152]{0:T(1024)S(1)} %sub.44), kind=kOutput, calls=%fused_computation.15 | convolution fusion | flops 1209073664 | bytes 3412480 | tf_op jit(solution)/shard_map/dot_general | solution.py:493
  212.4 0.3 reduce.3
  212.8 1.2 select_reduce_fusion
  214.0 16.8 %shard_map.79 = (bf16[128,4096]{1,0:T(8,128)(2,1)}, f32[8,128]{1,0:T(8,128)}) custom-call(bf16[4,128,1024]{2,1,0:T(8,128)(2,1)} %bitcast.45, f32[8,128]{1,0:T(8,128)} %bitcast.57), custom_call_target="tpu_custom_call" | custom-call | tf_op jit(solution)/shard_map/pallas_call | solution.py:402
  230.8 2.3 copy.30
  233.1 1.3 copy.31
  (20 shorter events, 0.7 us)
Async XLA Ops:
  32.1 4.2 %copy-start = (bf16[1,1024,2,384]{3,2,1,0:T(2,128)(2,1)S(1)}, bf16[1,1024,2,384]{3,2,1,0:T(2,128)(2,1)}, u32[]{:S(2)}) copy-start(bf16[1,1024,2,384]{3,2,1,0:T(2,128)(2,1)} %param.9) | copy-start | bytes 4718596
  36.3 6.9 %slice-start = ((s8[6291456]{0:T(1024)(128)(4,1)}), s8[4194304]{0:T(1024)(128)(4,1)S(1)}, s32[]{:S(2)}) async-start(s8[6291456]{0:T(1024)(128)(4,1)} %bitcast.40), calls=%async_computation | async-start | bytes 8388608
  38.5 4.7 %slice-start.1 = ((s8[6291456]{0:T(1024)(128)(4,1)}), s8[2097152]{0:T(1024)(128)(4,1)S(1)}, s32[]{:S(2)}) async-start(s8[6291456]{0:T(1024)(128)(4,1)} %bitcast.40), calls=%async_computation.1 | async-start | bytes 4194304
  208.0 4.3 %copy-start.1 = (f32[8,144,1]{2,1,0:T(8,128)S(1)}, f32[8,144,1]{2,1,0:T(8,128)}, u32[]{:S(2)}) copy-start(f32[8,144,1]{2,1,0:T(8,128)} %get-tuple-element.11) | copy-start | bytes 13828

commit v3 on v2

--- a/solution.py
+++ b/solution.py
@@ -206,6 +206,29 @@
     )(part)
 
 
+def plan(n_exp):
+    half = n_exp // 2
+    near = list(range(half))
+    order = [("send", k) for k in range(1, half + 2)]
+    order += [("spread", 0), ("spread", 1), ("turn", 0), ("compute", 0)]
+    order += [("spread", k) for k in near[2:]] + [("send", k) for k in range(half + 2, n_exp)]
+    order += [("turn", 1), ("compute", 1), ("hand", 0)] + [("turn", k) for k in near[2:]]
+    for k in near[2:]:
+        order += [("compute", k), ("hand", k - 1)]
+    order += [("hand", half - 1)]
+    before = near
+    for i in range(half, n_exp, 2):
+        j = i + 1
+        order += [("spread", i), ("spread", j)] + [("give", k) for k in before]
+        order += [("turn", i), ("turn", j), ("compute", i)]
+        if j < n_exp - 1:
+            order += [("compute", j), ("hand", i), ("hand", j)]
+        else:
+            order += [("hand", i), ("compute", j), ("hand", j)]
+        before = [i, j]
+    return order + [("give", k) for k in before]
+
+
 def expert_kernel(
     n_exp, out, gate, up, weight, down, mixing, arrived, score,
     fetched, both, part, near, sum1, far, sum2,
@@ -217,7 +240,6 @@
     across, beside = (g, flip(s, 2)), (g, flip(s, 1))
     own, theirs = columns(s, width), columns(flip(s, 2), width)
     greet([(flip(g, k), s) for k in range(1, n_exp)] + [across, beside])
-    half = n_exp // 2
     place = [flip(g, k) for k in range(n_exp)]
     first = pltpu.make_async_copy(out.at[g], fetched.at[g, :, own], local.at[0])
     first.start()
@@ -308,30 +330,10 @@
             last[k] = pltpu.make_async_copy(sum2.at[e], arrived.at[g], local.at[1])
         last[k].start()
 
-    batches = [list(range(half))] + [list(range(k, k + 2)) for k in range(half, n_exp, 2)]
-    for k in batches[1]:
-        send(k)
-    for k in batches[0][1:]:
-        send(k)
-    previous = []
-    for i, batch in enumerate(batches):
-        for k in batch:
-            spread(k)
-        if 0 < i < len(batches) - 1:
-            for k in batches[i + 1]:
-                send(k)
-        for k in previous:
-            give(k)
-        for k in batch:
-            turn(k)
-        for j, k in enumerate(batch):
-            compute(k)
-            if j:
-                hand(batch[j - 1])
-        hand(batch[-1])
-        previous = batch
-    for k in previous:
-        give(k)
+    steps = {"send": send, "spread": spread, "turn": turn}
+    steps.update({"compute": compute, "hand": hand, "give": give})
+    for step, k in plan(n_exp):
+        steps[step](k)
     for k in range(n_exp):
         if k:
             sends[k].wait_send()
@@ -457,7 +459,7 @@
         take, group.reshape(group_tok, width), preferred_element_type=jnp.float32
     ).astype(jnp.bfloat16)
     outgoing = outgoing.reshape(n_exp, slot_most, width)
-    if slot_most % 16 == 0:
+    if slot_most % 16 == 0 and n_exp >= 4:
         arrived, score_part = expert(
             n_exp,
             n_seq,

time: 235 us -> 226 us (0.962)
  Pallas kernels: 197 us -> 188 us
    pallas_call x1, Pallas kernels: 161 us -> 152 us  [expert(): pl.pallas_call(functools.partial(expert_kernel, n_exp), out_shape=(jax.Sh...]
where the time goes in v3:
time: 226 us; the launch traced here: 225 us
  Pallas kernels  188 us (83%)
  matrix products  13.2 us (6%)
  other arithmetic  11.8 us (5%)
  local copies, waits for them, and re-layouts  11.6 us (5%)
    pallas_call x1, Pallas kernels, expert(): pl.pallas_call(functools.partial(expert_kernel, n_exp), out_shape=(jax.Sh...  152 us
    pallas_call x1, Pallas kernels, exchange(): pl.pallas_call(functools.partial(exchange_kernel, n_exp, n_seq), out_shap...  19.2 us
    pallas_call x1, Pallas kernels, regroup(): pl.pallas_call(functools.partial(regroup_kernel, n_seq), out_shape=(jax.S...  16.8 us
    unnamed x12, local copies, waits for them, and re-layouts  7.41 us
    another operation x4, other arithmetic  4.86 us
    dot_general x2, matrix products, padded(): return jnp.dot(place_one, x, preferred_element_type=jnp.float32)  4.63 us

profile of v3, /device:TPU:8, one launch (start us, length us, event | category | flops | bytes accessed | tf_op | source)
XLA Modules:
  0.0 225.3 jit_solution(4469857621037178778)
XLA Ops:
  0.6 0.7 and_select_fusion
  1.4 2.3 %reduce-window.16 = s32[8,8,128]{2,1,0:T(8,128)S(1)} reduce-window(s32[8,8,128]{2,1,0:T(8,128)S(1)} %fusion.11, s32[]{:T(128)} %constant.35.clone.1), window={size=1x1x128 pad=0_0x0_0x127_0}, to_apply=%region_3.4 | reduce-window | flops 1040384 | bytes 65540 | tf_op jit(solution)/shard_map/reduce-window.2
  3.6 0.3 slice_reduce_fusion
  4.2 0.7 multiply_add_fusion
  4.9 1.2 select_reduce_fusion.1
  6.1 1.3 reshape.139.weight
  7.4 19.2 %shard_map.77 = (s32[8,8,128]{2,1,0:T(8,128)}, bf16[4,128,1024]{2,1,0:T(8,128)(2,1)}) custom-call(s32[8,128]{1,0:T(8,128)} %bitcast.48, bf16[128,4096]{1,0:T(8,128)(2,1)} %grad.1), custom_call_target="tpu_custom_call" | custom-call | tf_op jit(solution)/shard_map/pallas_call | solution.py:68
  26.6 0.8 add_bitcast_fusion
  27.3 0.8 fusion.12
  28.1 2.3 %reduce-window.14 = s32[8,8,128]{2,1,0:T(8,128)S(1)} reduce-window(s32[8,8,128]{2,1,0:T(8,128)S(1)} %get-tuple-element.14, s32[]{:T(128)} %constant.35.clone.1), window={size=1x1x128 pad=0_0x0_0x127_0}, to_apply=%region_0.1 | reduce-window | flops 1040384 | bytes 65540 | tf_op jit(solution)/shard_map/reduce-window
  30.4 0.3 slice_reduce_fusion.1
  30.9 1.1 select_reduce_fusion.2
  32.1 4.2 %convolution_convert_fusion = bf16[1152,1024]{1,0:T(8,128)(2,1)} fusion(bf16[512,1024]{1,0:T(8,128)(2,1)} %bitcast.64, s32[1152]{0:T(1024)S(1)} %sub.44), kind=kOutput, calls=%fused_computation.8 | convolution fusion | flops 1209729024 | bytes 3412480 | tf_op jit(solution)/shard_map/dot_general | solution.py:458
  36.3 2.2 fusion.13
  38.6 2.3 %fusion.4 = bf16[1152,384]{1,0:T(8,128)(2,1)} fusion(s32[1024]{0:T(1024)S(1)} %bitcast.50, bf16[1,1024,1,384]{3,2,1,0:T(2,128)(2,1)S(1)} %get-tuple-element.16), kind=kOutput, calls=%fused_computation.10 | convolution fusion | flops 907591680 | bytes 1675264 | tf_op jit(solution)/shard_map/dot_general | solution.py:443
  40.9 2.3 %fusion.3 = bf16[1152,384]{1,0:T(8,128)(2,1)} fusion(s32[1024]{0:T(1024)S(1)} %bitcast.51, bf16[1,1024,1,384]{3,2,1,0:T(2,128)(2,1)S(1)} %get-tuple-element.17), kind=kOutput, calls=%fused_computation.9 | convolution fusion | flops 907591680 | bytes 1675264 | tf_op jit(solution)/shard_map/dot_general | solution.py:443
  43.2 3.8 %copy.19 = bf16[512,8,2,384]{3,1,2,0:T(8,128)(2,1)} copy(bf16[512,8,2,384]{3,2,1,0:T(2,128)(2,1)S(1)} %bitcast.42) | data formatting | bytes 12582912
  47.0 152.0 %shard_map.78 = (bf16[8,144,1024]{2,1,0:T(8,128)(2,1)}, f32[8,144,1]{2,1,0:T(8,128)}) custom-call(bf16[8,144,1024]{2,1,0:T(8,128)(2,1)} %bitcast.44, bf16[8,144,384]{2,1,0:T(8,128)(2,1)} %bitcast.47, bf16[8,144,384]{2,1,0:T(8,128)(2,1)} %bitcast.46, f32[8,144,1]{2,1,0:T(8,128)} %reshape.139.weight, bf16[384,4096]{1,0:T(8,128)(2,1)} %bitcast.43, ...), custom_call_target="tpu_custom_call" | custom-call | tf_op jit(solution)/shard_map/pallas_call | solution.py:355
  199.0 4.3 %fusion.8 = bf16[512,1024]{1,0:T(8,128)(2,1)} fusion(bf16[1152,1024]{1,0:T(8,128)(2,1)} %bitcast.63, s32[1152]{0:T(1024)S(1)} %sub.44), kind=kOutput, calls=%fused_computation.15 | convolution fusion | flops 1209073664 | bytes 3412480 | tf_op jit(solution)/shard_map/dot_general | solution.py:495
  203.4 0.3 reduce.3
  203.8 1.2 select_reduce_fusion
  205.0 16.8 %shard_map.79 = (bf16[128,4096]{1,0:T(8,128)(2,1)}, f32[8,128]{1,0:T(8,128)}) custom-call(bf16[4,128,1024]{2,1,0:T(8,128)(2,1)} %bitcast.45, f32[8,128]{1,0:T(8,128)} %bitcast.57), custom_call_target="tpu_custom_call" | custom-call | tf_op jit(solution)/shard_map/pallas_call | solution.py:404
  221.8 2.3 %copy.30 = bf16[128,4096]{1,0:T(8,128)(2,1)} copy(bf16[128,4096]{1,0:T(8,128)(2,1)} %get-tuple-element.22) | data formatting | bytes 2097152
  224.1 1.3 copy.31
  (20 shorter events, 0.7 us)
Async XLA Ops:
  32.1 4.2 %copy-start = (bf16[1,1024,2,384]{3,2,1,0:T(2,128)(2,1)S(1)}, bf16[1,1024,2,384]{3,2,1,0:T(2,128)(2,1)}, u32[]{:S(2)}) copy-start(bf16[1,1024,2,384]{3,2,1,0:T(2,128)(2,1)} %param.9) | copy-start | bytes 4718596
  36.3 6.9 %slice-start = ((s8[6291456]{0:T(1024)(128)(4,1)}), s8[4194304]{0:T(1024)(128)(4,1)S(1)}, s32[]{:S(2)}) async-start(s8[6291456]{0:T(1024)(128)(4,1)} %bitcast.40), calls=%async_computation | async-start | bytes 8388608
  38.5 4.7 %slice-start.1 = ((s8[6291456]{0:T(1024)(128)(4,1)}), s8[2097152]{0:T(1024)(128)(4,1)S(1)}, s32[]{:S(2)}) async-start(s8[6291456]{0:T(1024)(128)(4,1)} %bitcast.40), calls=%async_computation.1 | async-start | bytes 4194304
  199.0 4.3 %copy-start.1 = (f32[8,144,1]{2,1,0:T(8,128)S(1)}, f32[8,144,1]{2,1,0:T(8,128)}, u32[]{:S(2)}) copy-start(f32[8,144,1]{2,1,0:T(8,128)} %get-tuple-element.11) | copy-start | bytes 13828
